TPU v7x, 256 devices: a whole 4x4x8 slice. The times are simulated.
256 devices in a mesh: seq: 64 (over y_lo, z, x), tp: 4 (over y_hi, core).
Axes of the slice: x: 4, y: 4 (y_hi: 2, y_lo: 2; y = y_hi * 2 + y_lo), z: 8, core: 2. Of those that a mesh axis runs over, the one named last changes fastest.
Arguments:
- queries: bfloat16 [16384, 1024], P('seq', 'tp'), may hold values from -6 to 6
- keys: bfloat16 [16384, 1024], P('seq', 'tp'), may hold values from -6 to 6
- values: bfloat16 [16384, 1024], P('seq', 'tp'), may hold values from -6 to 6
- out_weight: bfloat16 [1024, 5120], P('tp'), may hold values from -0.375 to 0.375
- residual: bfloat16 [16384, 5120], P(('seq', 'tp')), may hold values from -3 to 3
- gate: float32 [5120], replicated, may hold values from 0.5 to 1.5
- block_mask: int32 [128, 128], replicated, may hold values from 0 to 1, as said below
Outputs:
- updated: bfloat16 [16384, 5120], P(('seq', 'tp'))
Inputs may be any that keep to these rules, and one draw needn't show every extreme that they name: block_mask[i, j] is 1 wherever |i - j| <= 4. Group the blocks by index of seq, 2 consecutive blocks to an index; where two indices lie more than 2 apart, the rows of one index's query blocks name at most one key block of the other index, and for indices exactly 3 apart this most is always reached.
All inputs are finite; a program needn't handle non-finite values.
Results may differ from a plain program's by a relative error of at most 0.012.
Values may be sent and summed in bfloat16 or wider, within the bound.
A program may use at most 128 MiB of HBM per device.

v0:
```python
import jax
import jax.numpy as jnp
from jax import lax
from jax.sharding import PartitionSpec as P

HD = 128
BLOCK = 128


NEGATIVE = -1e30


def attend(carry, query_heads, key_piece, value_piece, tile_mask, score_scale):
    old_top, old_total, old_summed = carry
    key_rows = key_piece.shape[0]
    query_rows = query_heads.shape[0]
    local_heads = query_heads.shape[1]
    head_size = query_heads.shape[2]
    key_heads = key_piece.reshape(key_rows, local_heads, head_size)
    value_heads = value_piece.reshape(key_rows, local_heads, head_size)
    scores = (
        jnp.einsum("qhd,khd->hqk", query_heads, key_heads, preferred_element_type=jnp.float32)
        * score_scale
    )
    query_tiles = tile_mask.shape[0]
    key_tiles = tile_mask.shape[1]
    allowed = jnp.broadcast_to(
        (tile_mask > 0)[:, None, :, None],
        (query_tiles, query_rows // query_tiles, key_tiles, key_rows // key_tiles),
    )
    allowed = allowed.reshape(query_rows, key_rows)[None, :, :]
    scores = jnp.where(allowed, scores, NEGATIVE)
    new_top = jnp.maximum(old_top, jnp.max(scores, axis=-1))
    weights = jnp.where(allowed, jnp.exp(scores - new_top[:, :, None]), 0.0)
    new_total = jnp.sum(weights, axis=-1)
    added = jnp.einsum(
        "hqk,khd->qhd",
        weights.astype(jnp.bfloat16),
        value_heads,
        preferred_element_type=jnp.float32,
    )
    return (new_top, new_total, added)


def shards(queries, keys, values, out_weight, residual, gate, block_mask):
    tok_rows = queries.shape[0]
    width = queries.shape[1]
    local_heads = width // HD
    my_blocks = tok_rows // BLOCK
    all_blocks = block_mask.shape[0]
    score_scale = 1.0 / HD**0.5
    seq_place = lax.axis_index("seq")
    query_heads = queries.reshape(tok_rows, local_heads, HD)
    start_carry = (
        jnp.full((local_heads, tok_rows), NEGATIVE, jnp.float32),
        jnp.zeros((local_heads, tok_rows), jnp.float32),
        jnp.zeros((tok_rows, local_heads, HD), jnp.float32),
    )
    mask_rows = lax.dynamic_slice(
        block_mask, (seq_place * my_blocks, jnp.int32(0)), (my_blocks, all_blocks)
    )
    key_piece = lax.all_gather(keys, "seq", axis=0, tiled=True)
    value_piece = lax.all_gather(values, "seq", axis=0, tiled=True)
    row_top, totals, summed = attend(
        start_carry, query_heads, key_piece, value_piece, mask_rows, score_scale
    )
    attended = (
        (summed / jnp.transpose(totals)[:, :, None]).reshape(tok_rows, width).astype(jnp.bfloat16)
    )
    branch = lax.psum_scatter(
        jnp.dot(attended, out_weight, preferred_element_type=jnp.float32).astype(jnp.bfloat16),
        "tp",
        scatter_dimension=0,
        tiled=True,
    ).astype(jnp.float32)
    return (residual.astype(jnp.float32) + gate[None, :] * branch).astype(jnp.bfloat16)


def solution(mesh):
    return jax.shard_map(
        shards,
        mesh=mesh,
        in_specs=(
            P("seq", "tp"),
            P("seq", "tp"),
            P("seq", "tp"),
            P("tp", None),
            P(("seq", "tp"), None),
            P(),
            P(),
        ),
        out_specs=P(("seq", "tp"), None),
        check_vma=False,
    )
```

profile of v0, /device:TPU:1, one launch (start us, length us, event | category | flops | bytes accessed | tf_op | source)
XLA Modules:
  0.0 676.6 jit_solution(8116730190612022189)
XLA Ops:
  6.5 0.0 copy-start
  6.5 0.0 copy-start.3
  6.5 0.0 all-gather.3.cloned.1.call-start
  6.5 1.8 copy.10
  8.4 0.0 all-gather.3.cloned.1.call-update
  8.4 0.0 all-gather.5.cloned.1.call-start
  8.4 0.7 all-gather.5.cloned.1.call-update
  9.1 0.0 reduce-scatter.2.cloned.1.call-start
  9.2 0.7 dynamic-slice_compare_fusion
  9.9 2.2 broadcast_in_dim.32
  12.1 19.1 %copy.24 = pred[32,8,128,128]{3,1,2,0:T(8,128)(4,1)} copy(pred[32,8,128,128]{3,2,1,0:T(8,128)(4,1)S(1)} %bitcast.31) | data formatting | bytes 8388608
  31.2 211.7 %all-gather.3.cloned.1.call-done = bf16[16384,256]{0,1:T(8,128)(2,1)} async-done(((bf16[256,256]{0,1:T(8,128)(2,1)}), bf16[16384,256]{0,1:T(8,128)(2,1)}) %all-gather.3.cloned.1.call-update) | async-done | bytes 8388624 | tf_op jit(solution)/shard_map/all_gather | solution.py:62
  242.9 0.0 copy-done.3
  242.9 19.4 %fusion = (f32[2,256]{1,0:T(2,128)S(1)}, f32[2,256,16384]{2,1,0:T(8,128)}) fusion(pred[256,16384]{1,0:T(8,128)(4,1)} %bitcast.28, bf16[16384,2,128]{0,2,1:T(8,128)(2,1)} %bitcast.35, bf16[256,256]{1,0:T(8,128)(2,1)S(1)} %copy-done.3), kind=kOutput, calls=%fused_computation.2 | convolution fusion | flops 2172648960 | bytes 46270464 | tf_op jit(solution)/shard_map/qhd,khd->hqk/dot_general | solution.py:22
  262.3 16.3 %fusion.1 = f32[2,256]{1,0:T(2,128)S(1)} fusion(f32[2,256,16384]{2,1,0:T(8,128)} %get-tuple-element.6, f32[2,256]{1,0:T(2,128)S(1)} %broadcast_maximum_fusion, pred[256,16384]{1,0:T(8,128)(4,1)} %bitcast.29), kind=kLoop, calls=%fused_computation.3 | loop fusion | flops 41942528 | bytes 37752832 | tf_op jit(solution)/shard_map/reduce_sum | solution.py:35
  278.6 273.0 %all-gather.5.cloned.1.call-done = bf16[16384,256]{1,0:T(8,128)(2,1)} async-done(((bf16[256,256]{1,0:T(8,128)(2,1)}), bf16[16384,256]{1,0:T(8,128)(2,1)}) %all-gather.5.cloned.1.call-update) | async-done | bytes 8388624 | tf_op jit(solution)/shard_map/all_gather | solution.py:63
  551.6 11.9 %copy.13 = bf16[16384,256]{0,1:T(8,128)(2,1)} copy(bf16[16384,256]{1,0:T(8,128)(2,1)} %all-gather.5.cloned.1.call-done) | data formatting | bytes 16777216 | tf_op jit(solution)/shard_map/all_gather | solution.py:63
  563.5 0.0 copy-start.2
  563.5 17.3 %fusion.12 = bf16[256,2,128]{0,2,1:T(8,128)(2,1)S(1)} fusion(bf16[16384,2,128]{0,2,1:T(8,128)(2,1)} %bitcast.32, f32[2,256,16384]{2,1,0:T(8,128)} %get-tuple-element.6, f32[2,256]{1,0:T(2,128)S(1)} %broadcast_maximum_fusion, pred[256,16384]{1,0:T(8,128)(4,1)} %bitcast.30, f32[256,2]{0,1:T(2,128)S(1)} %bitcast.34), kind=kOutput, calls=%fused_computation.12 | convolution fusion | flops 2189557760 | bytes 46272512 | tf_op jit(solution)/shard_map/hqk,khd->qhd/dot_general | solution.py:36
  580.9 0.0 copy-start.1
  580.9 0.0 copy-done
  580.9 2.4 convolution_convert_fusion
  583.3 0.0 reduce-scatter.2.cloned.1.call-update
  583.3 84.6 %reduce-scatter.2.cloned.1.call-done = bf16[64,5120]{1,0:T(8,128)(2,1)} async-done(((bf16[256,5120]{1,0:T(8,128)(2,1)}), bf16[64,5120]{1,0:T(8,128)(2,1)}) %reduce-scatter.2.cloned.1.call-update) | async-done | bytes 655376 | tf_op jit(solution)/shard_map/reduce_scatter | solution.py:70
  667.9 0.0 copy-done.2
  667.9 0.0 copy-done.1
  667.9 2.1 add_convert_fusion
  (1 shorter events, 0.0 us)
Async XLA Ops:
  6.5 574.3 %copy-start = (bf16[256,5120]{1,0:T(8,128)(2,1)S(1)}, bf16[256,5120]{1,0:T(8,128)(2,1)}, u32[]{:S(2)}) copy-start(bf16[256,5120]{1,0:T(8,128)(2,1)} %param.10) | copy-start | bytes 7864324
  6.5 236.4 %copy-start.3 = (bf16[256,256]{1,0:T(8,128)(2,1)S(1)}, bf16[256,256]{1,0:T(8,128)(2,1)}, u32[]{:S(2)}) copy-start(bf16[256,256]{1,0:T(8,128)(2,1)} %param.7) | copy-start | bytes 393220
  6.5 236.4 %all-gather.3.cloned.1.call-start = ((), (), s32[]{:S(2)}) async-start(), calls=%async_computation.1 | async-start | bytes 8519680 | tf_op jit(solution)/shard_map/all_gather | solution.py:62
  8.4 543.2 %all-gather.5.cloned.1.call-start = ((), (), s32[]{:S(2)}) async-start(), calls=%async_computation.2 | async-start | bytes 8519680 | tf_op jit(solution)/shard_map/all_gather | solution.py:63
  9.1 658.8 %reduce-scatter.2.cloned.1.call-start = ((), (), s32[]{:S(2)}) async-start(), calls=%async_computation.3 | async-start | bytes 3276800 | tf_op jit(solution)/shard_map/reduce_scatter | solution.py:70
  563.5 104.4 %copy-start.2 = (f32[5120]{0:T(1024)S(1)}, f32[5120]{0:T(1024)}, u32[]{:S(2)}) copy-start(f32[5120]{0:T(1024)} %param.12) | copy-start | bytes 61444
  580.9 87.1 %copy-start.1 = (bf16[64,5120]{1,0:T(8,128)(2,1)S(1)}, bf16[64,5120]{1,0:T(8,128)(2,1)}, u32[]{:S(2)}) copy-start(bf16[64,5120]{1,0:T(8,128)(2,1)} %param.11) | copy-start | bytes 1966084
Sparse Core Ops, SparseCore 0:
  9.0 233.7 all-gather.2
  244.7 306.9 all-gather.4
  583.4 84.4 reduce-scatter.1
where the time goes:
time: 677 us
  waiting for transfers between devices  570 us (84%)
  matrix products  39.1 us (6%)
  local copies, waits for them, and re-layouts  35 us (5%)
  other arithmetic  19.1 us (3%)
  between operations  13.1 us (2%)
    all_gather x1, waiting for transfers between devices, shards(): value_piece = lax.all_gather(values, 'seq', axis=0, tiled=True)  273 us
    all_gather x1, waiting for transfers between devices, shards(): key_piece = lax.all_gather(keys, 'seq', axis=0, tiled=True)  212 us
    reduce_scatter x1, waiting for transfers between devices, shards(): lax.psum_scatter(jnp.dot(attended, out_weight, preferred_element_type=jnp...  84.6 us
    unnamed x10, local copies, waits for them, and re-layouts  21 us
    dot_general x1, matrix products, attend(): jnp.einsum('qhd,khd->hqk', query_heads, key_heads, preferred_element_type...  19.4 us
    dot_general x1, matrix products, attend(): jnp.einsum('hqk,khd->qhd', weights.astype(jnp.bfloat16), value_heads, pre...  17.3 us
    reduce_sum x1, other arithmetic, attend(): new_total = jnp.sum(weights, axis=-1)  16.3 us
  transfers between devices with their start and end apart: 3, of which 3 were waited for; matrix products, arithmetic and copies ran while one was open for 9% of the time, Pallas kernels for 0%

commit v1 on v0

v1 whole, which is shorter than its diff:
```python
import functools

import jax
import jax.numpy as jnp
from jax import lax
from jax.experimental import pallas as pl
from jax.experimental.pallas import tpu as pltpu
from jax.sharding import PartitionSpec as P

HD = 128
BLOCK = 128
LOW = -1e30
BIG = 1e30
EXP2_SCALE = 1.4426950408889634 / HD**0.5
MESH = pl.DeviceIdType.MESH

NX = 4
NZ = 8
HALF = NX * NZ


def wait_bytes(ref, sem):
    pltpu.make_async_copy(ref, ref, sem).wait()


def attention_kernel(
    q_ref, k_ref, v_ref, mask_ref, att_ref,
    mask_s, qin, kv, acc, top, tot, o_send, o_recv, s_send, s_recv, att_send, att_buf,
    mask_sem, a_send, a_recv, q_send, q_recv, ring_send, ring_recv, sib_send,
    os_send, os_recv, d_send, d_recv,
):
    s = lax.axis_index("seq")
    t = lax.axis_index("tp")
    y_lo = s // HALF
    z = (s // NX) % NZ
    x = s % NX
    y_hi = t // 2
    c = t % 2
    plane = y_lo * HALF + z * NX
    z_up = y_lo * HALF + ((z + 1) % NZ) * NX + x
    z_down = y_lo * HALF + ((z + NZ - 1) % NZ) * NX + x
    partner = (1 - y_lo) * HALF + z * NX + x

    barrier = pltpu.get_barrier_semaphore()
    member = y_hi * 8 + x * 2 + c

    def greet(o, carry):
        m = (member + o) % 16
        pl.semaphore_signal(
            barrier, inc=1, device_id=(plane + (m // 2) % 4, (m // 8) * 2 + m % 2), device_id_type=MESH
        )
        return carry

    lax.fori_loop(1, 16, greet, 0)
    for other in (z_up, z_down, partner):
        pl.semaphore_signal(barrier, inc=1, device_id=(other, t), device_id_type=MESH)

    mask_copies = []
    for n, half in enumerate((y_lo, 1 - y_lo)):
        rows = pl.ds(pl.multiple_of((half * NZ + z) * 8, 8), 8)
        copy = pltpu.make_async_copy(mask_ref.at[rows], mask_s.at[n], mask_sem.at[n])
        copy.start()
        mask_copies.append(copy)
    top[...] = jnp.full(top.shape, LOW, jnp.float32)
    tot[...] = jnp.zeros(tot.shape, jnp.float32)
    acc[...] = jnp.zeros(acc.shape, jnp.float32)
    pl.semaphore_wait(barrier, 18)

    my_slot = z * NX + x
    for jj in range(2):
        j = 2 * c + jj
        columns = pl.ds(jj * HD, HD)
        pieces = ((k_ref, kv.at[my_slot, 0]), (v_ref, kv.at[my_slot, 1]), (q_ref, qin.at[x % 2]))
        for n, (src, dst) in enumerate(pieces):
            @pl.when(j != x)
            def _():
                pltpu.make_async_remote_copy(
                    src.at[:, columns], dst, a_send.at[jj, n], a_recv.at[x % 2, n],
                    device_id=(plane + j, y_hi * 2 + x // 2), device_id_type=MESH,
                ).start()

            @pl.when(j == x)
            def _():
                pltpu.make_async_copy(src.at[:, columns], dst, a_recv.at[x % 2, n]).start()

    def ring(idx, direction):
        pltpu.make_async_remote_copy(
            kv.at[idx], kv.at[idx], ring_send.at[direction, idx], ring_recv.at[idx],
            device_id=(z_up if direction == 0 else z_down, t), device_id_type=MESH,
        ).start()

    def to_sibling(idx):
        pltpu.make_async_remote_copy(
            kv.at[idx], kv.at[idx], sib_send.at[idx], ring_recv.at[idx],
            device_id=(s, y_hi * 2 + 1 - c), device_id_type=MESH,
        ).start()

    for e in range(2):
        idx = z * NX + 2 * c + e
        for n in range(2):
            wait_bytes(kv.at[idx, n], a_recv.at[e, n])
        ring(idx, 0)
        ring(idx, 1)
        to_sibling(idx)
    for i in range(2):
        wait_bytes(qin.at[i], a_recv.at[i, 2])
        pltpu.make_async_remote_copy(
            qin.at[i], qin.at[2 + i], q_send.at[i], q_recv.at[i],
            device_id=(partner, t), device_id_type=MESH,
        ).start()
    for copy in mask_copies:
        copy.wait()
    for i in range(2):
        wait_bytes(qin.at[2 + i], q_recv.at[i])

    lane = lax.broadcasted_iota(jnp.int32, (1, 2 * BLOCK), 1)

    def compute(zz, cc):
        b0 = zz * NX + 2 * cc
        g0 = y_lo * HALF + b0
        near = jnp.int32(0)
        for grp, half in enumerate((y_lo, 1 - y_lo)):
            for i in range(2):
                a = half * HALF + z * NX + 2 * c + i
                for e in range(2):
                    gap = a - (g0 + e)
                    near = near | ((gap <= 2) & (gap >= -2)).astype(jnp.int32)

        def one_round(rr, carry):
            for q in range(4):
                grp, i = q // 2, q % 2
                row = (2 * c + i) * 2
                halves_k, halves_v, conds = [], [], []
                for e in range(2):
                    col = 2 * (g0 + e)
                    m00 = mask_s[grp, row, col]
                    m10 = mask_s[grp, row + 1, col]
                    m01 = mask_s[grp, row, col + 1]
                    m11 = mask_s[grp, row + 1, col + 1]
                    block = (m01 | m11) ^ rr
                    upper = block != 0
                    allow0 = jnp.where(upper, m01, m00)
                    allow1 = jnp.where(upper, m11, m10)
                    conds.append(jnp.where(lane < BLOCK, allow0, allow1) != 0)
                    halves_k.append(jnp.where(upper, kv[b0 + e, 0, BLOCK:, :], kv[b0 + e, 0, :BLOCK, :]))
                    halves_v.append(jnp.where(upper, kv[b0 + e, 1, BLOCK:, :], kv[b0 + e, 1, :BLOCK, :]))
                kk = jnp.concatenate(halves_k, axis=0)
                vv = jnp.concatenate(halves_v, axis=0)
                scores = lax.dot_general(
                    kk, qin[q], (((1,), (1,)), ((), ())), preferred_element_type=jnp.float32
                )
                parts = (scores[:BLOCK], scores[BLOCK:])
                old = top[q]
                new = old
                for part, cond in zip(parts, conds):
                    new = jnp.maximum(new, jnp.where(cond, jnp.max(part, axis=0, keepdims=True), LOW))
                alpha = jnp.exp2((old - new) * EXP2_SCALE)
                scaled = new * EXP2_SCALE
                total = tot[q] * alpha
                weights = []
                for part, cond in zip(parts, conds):
                    weight = jnp.exp2(part * EXP2_SCALE - jnp.where(cond, scaled, BIG))
                    total = total + jnp.sum(weight, axis=0, keepdims=True)
                    weights.append(weight.astype(jnp.bfloat16))
                top[q] = new
                tot[q] = total
                added = lax.dot_general(
                    vv, jnp.concatenate(weights, axis=0), (((0,), (0,)), ((), ())),
                    preferred_element_type=jnp.float32,
                )
                acc[q] = acc[q] * alpha + added
            return carry

        lax.fori_loop(0, 1 + near, one_round, 0)

    def step(h, carry):
        u = h // 2
        e = h % 2
        r = (u + 1) // 2
        up = (u % 2 == 1).astype(jnp.int32)
        zz = (z + NZ + jnp.where(up == 1, -r, r)) % NZ
        idx = zz * NX + 2 * c + e

        @pl.when(u > 0)
        def _():
            wait_bytes(kv.at[idx], ring_recv.at[idx])
            to_sibling(idx)

            @pl.when((up == 1) & (r < 4 - e))
            def _():
                ring(idx, 0)

            @pl.when((up == 0) & (r < 3 + e))
            def _():
                ring(idx, 1)

        @pl.when(h > 0)
        def _():
            pu = jnp.where(e == 0, u - 1, u)
            pr = (pu + 1) // 2
            pz = (z + NZ + jnp.where(pu % 2 == 1, -pr, pr)) % NZ
            pc = jnp.where(e == 0, 1 - c, c)

            @pl.when(e == 0)
            def _():
                for n in range(2):
                    slot = pz * NX + 2 * pc + n
                    wait_bytes(kv.at[slot], ring_recv.at[slot])

            compute(pz, pc)

        return carry

    lax.fori_loop(0, 16, step, 0)
    last = (z + 4) % NZ
    for n in range(2):
        slot = last * NX + 2 * (1 - c) + n
        wait_bytes(kv.at[slot], ring_recv.at[slot])
    compute(last, 1 - c)

    for i in range(2):
        o_send[i] = acc[2 + i].astype(jnp.bfloat16)
        s_send[pl.ds(2 * i, 1), :] = top[2 + i]
        s_send[pl.ds(2 * i + 1, 1), :] = tot[2 + i]
    partial = []
    for n, (src, dst) in enumerate(((s_send, s_recv), (o_send, o_recv))):
        copy = pltpu.make_async_remote_copy(
            src, dst, os_send.at[n], os_recv.at[n], device_id=(partner, t), device_id_type=MESH
        )
        copy.start()
        partial.append(copy)
    for copy in partial:
        copy.wait_recv()
    for i in range(2):
        top_one, tot_one = top[i], tot[i]
        top_two, tot_two = s_recv[pl.ds(2 * i, 1), :], s_recv[pl.ds(2 * i + 1, 1), :]
        both = jnp.maximum(top_one, top_two)
        one = jnp.exp2((top_one - both) * EXP2_SCALE)
        two = jnp.exp2((top_two - both) * EXP2_SCALE)
        total = tot_one * one + tot_two * two
        merged = (acc[i] * one + o_recv[i].astype(jnp.float32) * two) / total
        att_send[i] = merged.T.astype(jnp.bfloat16)

    head = y_hi * NX + x
    rows = att_buf.shape[1]
    for i in range(2):
        for other in range(4):
            src = att_send.at[i, pl.ds(other * rows, rows)]
            mine = (2 * c + i == x) & (t == other)

            @pl.when(jnp.logical_not(mine))
            def _():
                pltpu.make_async_remote_copy(
                    src, att_buf.at[head], d_send.at[i, other], d_recv.at[head],
                    device_id=(plane + 2 * c + i, other), device_id_type=MESH,
                ).start()

            @pl.when(mine)
            def _():
                pltpu.make_async_copy(src, att_buf.at[head], d_recv.at[head]).start()

    for h in range(8):
        wait_bytes(att_buf.at[h], d_recv.at[h])
    att_ref[...] = att_buf[...]

    for jj in range(2):
        @pl.when(2 * c + jj != x)
        def _():
            for n in range(3):
                wait_bytes(qin.at[0], a_send.at[jj, n])
    for i in range(2):
        wait_bytes(qin.at[i], q_send.at[i])
    for copy in partial:
        copy.wait_send()
    for i in range(2):
        for other in range(4):
            @pl.when(jnp.logical_not((2 * c + i == x) & (t == other)))
            def _():
                wait_bytes(att_buf.at[0], d_send.at[i, other])

    def drain(h, carry):
        u = h // 2
        e = h % 2
        r = (u + 1) // 2
        up = (u % 2 == 1).astype(jnp.int32)
        zz = (z + NZ + jnp.where(up == 1, -r, r)) % NZ
        idx = zz * NX + 2 * c + e
        wait_bytes(kv.at[idx], sib_send.at[idx])

        @pl.when((u == 0) | ((up == 1) & (r < 4 - e)))
        def _():
            wait_bytes(kv.at[idx], ring_send.at[0, idx])

        @pl.when((u == 0) | ((up == 0) & (r < 3 + e)))
        def _():
            wait_bytes(kv.at[idx], ring_send.at[1, idx])

        return carry

    lax.fori_loop(0, 16, drain, 0)


def shards(queries, keys, values, out_weight, residual, gate, block_mask):
    rows = residual.shape[0]
    toks = queries.shape[0]
    bf16, f32 = jnp.bfloat16, jnp.float32
    dma = pltpu.SemaphoreType.DMA
    att = pl.pallas_call(
        attention_kernel,
        out_shape=jax.ShapeDtypeStruct((8, rows, HD), bf16),
        in_specs=[pl.BlockSpec(memory_space=pl.ANY)] * 4,
        out_specs=pl.BlockSpec(memory_space=pltpu.VMEM),
        scratch_shapes=[
            pltpu.SMEM((2, 8, 128), jnp.int32),
            pltpu.VMEM((4, toks, HD), bf16),
            pltpu.VMEM((HALF, 2, toks, HD), bf16),
            pltpu.VMEM((4, HD, toks), f32),
            pltpu.VMEM((4, 1, toks), f32),
            pltpu.VMEM((4, 1, toks), f32),
            pltpu.VMEM((2, HD, toks), bf16),
            pltpu.VMEM((2, HD, toks), bf16),
            pltpu.VMEM((8, toks), f32),
            pltpu.VMEM((8, toks), f32),
            pltpu.VMEM((2, toks, HD), bf16),
            pltpu.VMEM((8, rows, HD), bf16),
            dma((2,)), dma((2, 3)), dma((2, 3)), dma((2,)), dma((2,)),
            dma((2, HALF)), dma((HALF,)), dma((HALF,)),
            dma((2,)), dma((2,)), dma((2, 4)), dma((8,)),
        ],
        compiler_params=pltpu.CompilerParams(
            collective_id=0, has_side_effects=True, vmem_limit_bytes=32 * 1024 * 1024
        ),
        name="attend",
    )(queries, keys, values, block_mask)
    att = jnp.transpose(att, (1, 0, 2)).reshape(rows, 8 * HD)
    weight = lax.all_gather(out_weight, "tp", axis=0, tiled=True)
    branch = jnp.dot(att, weight, preferred_element_type=f32)
    return (residual.astype(f32) + gate[None, :] * branch).astype(bf16)


def solution(mesh):
    return jax.shard_map(
        shards,
        mesh=mesh,
        in_specs=(
            P("seq", "tp"),
            P("seq", "tp"),
            P("seq", "tp"),
            P("tp", None),
            P(("seq", "tp"), None),
            P(),
            P(),
        ),
        out_specs=P(("seq", "tp"), None),
        check_vma=False,
    )
```

time: 677 us -> 108 us (0.16)
  waiting for transfers between devices: 570 us -> 24.3 us
  Pallas kernels: 0 us -> 63.3 us
  local copies, waits for them, and re-layouts: 35 us -> 0.32 us
  matrix products: 39.1 us -> 6.76 us
  other arithmetic: 19.1 us -> 0 us
    all_gather x2 -> x1, waiting for transfers between devices: 485 us -> 23.6 us  [shards(): weight = lax.all_gather(out_weight, 'tp', axis=0, tiled=True)]
    reduce_scatter x1 -> x0, waiting for transfers between devices: 84.6 us -> none  [shards(): lax.psum_scatter(jnp.dot(attended, out_weight, preferred_element_type=jnp...]
    pallas_call x0 -> x1, Pallas kernels: none -> 63.3 us  [shards(): pl.pallas_call(attention_kernel, out_shape=jax.ShapeDtypeStruct((8, rows,...]
    dot_general x3 -> x1, matrix products: 39.1 us -> 6.76 us  [shards(): branch = jnp.dot(att, weight, preferred_element_type=f32)]
    unnamed x10 -> x12, local copies, waits for them, and re-layouts: 21 us -> 0.32 us
    reduce_sum x1 -> x0, other arithmetic: 16.3 us -> none  [attend(): new_total = jnp.sum(weights, axis=-1)]
    all_gather x1 -> x0, local copies, waits for them, and re-layouts: 11.9 us -> none  [shards(): value_piece = lax.all_gather(values, 'seq', axis=0, tiled=True)]
  transfers between devices with their start and end apart: 3 -> 1, of which waited for: 3 -> 1; matrix products, arithmetic and copies ran while one was open for 9% -> 0% of each run, Pallas kernels for 0% -> 59%
where the time goes in v1:
time: 108 us
  Pallas kernels  63.3 us (59%)
  waiting for transfers between devices  24.3 us (22%)
  between operations  13.4 us (12%)
  matrix products  6.76 us (6%)
    pallas_call x1, Pallas kernels, shards(): pl.pallas_call(attention_kernel, out_shape=jax.ShapeDtypeStruct((8, rows,...  63.3 us
    all_gather x1, waiting for transfers between devices, shards(): weight = lax.all_gather(out_weight, 'tp', axis=0, tiled=True)  23.6 us
    dot_general x1, matrix products, shards(): branch = jnp.dot(att, weight, preferred_element_type=f32)  6.76 us
  transfers between devices with their start and end apart: 1, of which 1 were waited for; matrix products, arithmetic and copies ran while one was open for 0% of the time, Pallas kernels for 59%

profile of v1, /device:TPU:1, one launch (start us, length us, event | category | flops | bytes accessed | tf_op | source)
XLA Modules:
  0.0 108.2 jit_solution(11938263087292856256)
XLA Ops:
  6.5 0.0 copy-start.3
  6.5 0.0 copy-start.2
  6.5 0.0 copy-start.1
  6.5 0.0 copy-start
  6.5 0.0 copy-start.5
  6.5 0.0 copy-start.4
  6.6 0.0 all-gather.2.cloned.1.call-start
  6.6 0.7 all-gather.2.cloned.1.call-update
  7.3 0.1 copy-done.3
  7.4 0.1 copy-done.2
  7.5 0.1 copy-done.1
  7.5 0.1 copy-done
  7.6 63.3 %attend.1 = bf16[8,64,128]{2,1,0:T(8,128)(2,1)S(1)} custom-call(bf16[256,256]{1,0:T(8,128)(2,1)S(1)} %copy-done, bf16[256,256]{1,0:T(8,128)(2,1)S(1)} %copy-done.1, bf16[256,256]{1,0:T(8,128)(2,1)S(1)} %copy-done.2, s32[128,128]{1,0:T(8,128)S(1)} %copy-done.3), custom_call_target="tpu_custom_call" | custom-call | tf_op jit(solution)/shard_map/attend/pallas_call | solution.py:308
  70.9 23.6 %all-gather.2.cloned.1.call-done = bf16[1024,5120]{1,0:T(8,128)(2,1)} async-done(((bf16[256,5120]{1,0:T(8,128)(2,1)}), bf16[1024,5120]{1,0:T(8,128)(2,1)}) %all-gather.2.cloned.1.call-update) | async-done | bytes 10485776 | tf_op jit(solution)/shard_map/all_gather | solution.py:336
  94.6 0.0 copy-done.5
  94.6 0.0 copy-done.4
  94.6 6.8 %fusion.1 = bf16[64,5120]{1,0:T(8,128)(2,1)} fusion(bf16[1024,5120]{1,0:T(8,128)(2,1)} %all-gather.2.cloned.1.call-done, bf16[64,5120]{1,0:T(8,128)(2,1)S(1)} %copy-done.4, f32[5120]{0:T(1024)S(1)} %copy-done.5, bf16[8,64,128]{2,1,0:T(8,128)(2,1)S(1)} %attend.1), kind=kOutput, calls=%fused_computation.2 | convolution fusion | flops 672399360 | bytes 11948032 | tf_op jit(solution)/shard_map/dot_general | solution.py:337
Async XLA Ops:
  6.5 0.8 copy-start.3
  6.5 0.9 copy-start.2
  6.5 1.0 copy-start.1
  6.5 1.1 copy-start
  6.5 88.1 %copy-start.5 = (f32[5120]{0:T(1024)S(1)}, f32[5120]{0:T(1024)}, u32[]{:S(2)}) copy-start(f32[5120]{0:T(1024)} %param.12) | copy-start | bytes 61444
  6.5 88.0 %copy-start.4 = (bf16[64,5120]{1,0:T(8,128)(2,1)S(1)}, bf16[64,5120]{1,0:T(8,128)(2,1)}, u32[]{:S(2)}) copy-start(bf16[64,5120]{1,0:T(8,128)(2,1)} %param.11) | copy-start | bytes 1966084
  6.6 88.0 %all-gather.2.cloned.1.call-start = ((), (), s32[]{:S(2)}) async-start(), calls=%async_computation | async-start | bytes 13107200 | tf_op jit(solution)/shard_map/all_gather | solution.py:336
Sparse Core Ops, SparseCore 0:
  9.2 85.3 all-gather.1

commit v2 on v1

--- a/solution.py
+++ b/solution.py
@@ -19,15 +19,22 @@
 HALF = NX * NZ
 
 
+W_PLAN = (
+    (2, 0, 1), (4, 1, 0), (5, 0, 2), (7, 1, 1), (8, 0, 3), (10, 1, 2), (11, 2, 0), (12, 2, 1), (13, 1, 3),
+)
+
+
 def wait_bytes(ref, sem):
     pltpu.make_async_copy(ref, ref, sem).wait()
 
 
 def attention_kernel(
-    q_ref, k_ref, v_ref, mask_ref, att_ref,
+    q_ref, k_ref, v_ref, w_ref, res_ref, gate_ref, mask_ref, out_ref,
     mask_s, qin, kv, acc, top, tot, o_send, o_recv, s_send, s_recv, att_send, att_buf,
+    wbuf, res, gate, branch,
     mask_sem, a_send, a_recv, q_send, q_recv, ring_send, ring_recv, sib_send,
     os_send, os_recv, d_send, d_recv,
+    local_sem, cross_send, w_recv, x_send, wsib_send, wsib_recv, own_send, own_recv,
 ):
     s = lax.axis_index("seq")
     t = lax.axis_index("tp")
@@ -40,6 +47,10 @@
     z_up = y_lo * HALF + ((z + 1) % NZ) * NX + x
     z_down = y_lo * HALF + ((z + NZ - 1) % NZ) * NX + x
     partner = (1 - y_lo) * HALF + z * NX + x
+    x_up = plane + (x + 1) % NX
+    x_down = plane + (x + NX - 1) % NX
+    sibling = y_hi * 2 + 1 - c
+    facing = (1 - y_hi) * 2 + c
 
     barrier = pltpu.get_barrier_semaphore()
     member = y_hi * 8 + x * 2 + c
@@ -54,6 +65,7 @@
     lax.fori_loop(1, 16, greet, 0)
     for other in (z_up, z_down, partner):
         pl.semaphore_signal(barrier, inc=1, device_id=(other, t), device_id_type=MESH)
+    pl.semaphore_signal(barrier, inc=1, device_id=(partner, facing), device_id_type=MESH)
 
     mask_copies = []
     for n, half in enumerate((y_lo, 1 - y_lo)):
@@ -64,24 +76,80 @@
     top[...] = jnp.full(top.shape, LOW, jnp.float32)
     tot[...] = jnp.zeros(tot.shape, jnp.float32)
     acc[...] = jnp.zeros(acc.shape, jnp.float32)
-    pl.semaphore_wait(barrier, 18)
+    local = []
+    for n, (src, dst) in enumerate(((w_ref, wbuf.at[t]), (res_ref, res), (gate_ref, gate))):
+        copy = pltpu.make_async_copy(src, dst, local_sem.at[n])
+        copy.start()
+        local.append(copy)
+    pl.semaphore_wait(barrier, 19)
 
     my_slot = z * NX + x
-    for jj in range(2):
+    pieces = ((k_ref, kv.at[my_slot, 0]), (v_ref, kv.at[my_slot, 1]), (q_ref, qin.at[x % 2]))
+    for jj, n in ((0, 0), (1, 0), (0, 1), (1, 1), (0, 2), (1, 2)):
         j = 2 * c + jj
+        src, dst = pieces[n]
         columns = pl.ds(jj * HD, HD)
-        pieces = ((k_ref, kv.at[my_slot, 0]), (v_ref, kv.at[my_slot, 1]), (q_ref, qin.at[x % 2]))
-        for n, (src, dst) in enumerate(pieces):
-            @pl.when(j != x)
-            def _():
-                pltpu.make_async_remote_copy(
-                    src.at[:, columns], dst, a_send.at[jj, n], a_recv.at[x % 2, n],
-                    device_id=(plane + j, y_hi * 2 + x // 2), device_id_type=MESH,
-                ).start()
-
-            @pl.when(j == x)
-            def _():
-                pltpu.make_async_copy(src.at[:, columns], dst, a_recv.at[x % 2, n]).start()
+
+        @pl.when(j != x)
+        def _():
+            pltpu.make_async_remote_copy(
+                src.at[:, columns], dst, a_send.at[jj, n], a_recv.at[x % 2, n],
+                device_id=(plane + j, y_hi * 2 + x // 2), device_id_type=MESH,
+            ).start()
+
+        @pl.when(j == x)
+        def _():
+            pltpu.make_async_copy(src.at[:, columns], dst, a_recv.at[x % 2, n]).start()
+
+    quarter = w_ref.shape[0] // NX
+    chunk = quarter // 4
+
+    def chunk_rows(qx, m):
+        return pl.ds(pl.multiple_of(qx * quarter + m * chunk, 8), chunk)
+
+    for m in range(4):
+        pltpu.make_async_remote_copy(
+            w_ref.at[chunk_rows(x, m)], wbuf.at[t, chunk_rows(x, m)], cross_send.at[m], w_recv.at[x * 4 + m],
+            device_id=(partner, facing), device_id_type=MESH,
+        ).start()
+
+    def w_piece(qx, m):
+        return wbuf.at[facing, chunk_rows(qx, m)]
+
+    def w_to(qx, m, direction):
+        piece = w_piece(qx, m)
+        pltpu.make_async_remote_copy(
+            piece, piece, x_send.at[direction, qx * 4 + m], w_recv.at[qx * 4 + m],
+            device_id=(x_up if direction == 0 else x_down, t), device_id_type=MESH,
+        ).start()
+
+    def w_sibling(qx, m):
+        piece = w_piece(qx, m)
+        pltpu.make_async_remote_copy(
+            piece, piece, wsib_send, wsib_recv, device_id=(s, sibling), device_id_type=MESH
+        ).start()
+
+    def w_first(m):
+        wait_bytes(w_piece(x, m), w_recv.at[x * 4 + m])
+        w_to(x, m, 0)
+        w_to(x, m, 1)
+        w_sibling(x, m)
+
+    def w_second(m):
+        below, above = (x + NX - 1) % NX, (x + 1) % NX
+        wait_bytes(w_piece(below, m), w_recv.at[below * 4 + m])
+        if m % 2 == 0:
+            w_to(below, m, 0)
+        w_sibling(below, m)
+        wait_bytes(w_piece(above, m), w_recv.at[above * 4 + m])
+        if m % 2 == 1:
+            w_to(above, m, 1)
+        w_sibling(above, m)
+
+    def w_third(m):
+        far = (x + 2) % NX
+        wait_bytes(w_piece(far, m), w_recv.at[far * 4 + m])
+        w_sibling(far, m)
 
     def ring(idx, direction):
         pltpu.make_async_remote_copy(
@@ -92,7 +160,7 @@
     def to_sibling(idx):
         pltpu.make_async_remote_copy(
             kv.at[idx], kv.at[idx], sib_send.at[idx], ring_recv.at[idx],
-            device_id=(s, y_hi * 2 + 1 - c), device_id_type=MESH,
+            device_id=(s, sibling), device_id_type=MESH,
         ).start()
 
     for e in range(2):
@@ -110,8 +178,7 @@
         ).start()
     for copy in mask_copies:
         copy.wait()
-    for i in range(2):
-        wait_bytes(qin.at[2 + i], q_recv.at[i])
+    w_first(0)
 
     lane = lax.broadcasted_iota(jnp.int32, (1, 2 * BLOCK), 1)
 
@@ -194,6 +261,22 @@
             def _():
                 ring(idx, 1)
 
+        own_rows = pl.ds(pl.multiple_of(h * chunk, 8), chunk)
+        pltpu.make_async_remote_copy(
+            w_ref.at[own_rows], wbuf.at[t, own_rows], own_send, own_recv,
+            device_id=(s, sibling), device_id_type=MESH,
+        ).start()
+
+        for at, event, m in W_PLAN:
+            @pl.when(h == at)
+            def _():
+                (w_first, w_second, w_third)[event](m)
+
+        @pl.when(h == 1)
+        def _():
+            for i in range(2):
+                wait_bytes(qin.at[2 + i], q_recv.at[i])
+
         @pl.when(h > 0)
         def _():
             pu = jnp.where(e == 0, u - 1, u)
@@ -218,32 +301,34 @@
         wait_bytes(kv.at[slot], ring_recv.at[slot])
     compute(last, 1 - c)
 
+    w_third(2)
+    w_third(3)
+
+    partial = []
     for i in range(2):
         o_send[i] = acc[2 + i].astype(jnp.bfloat16)
-        s_send[pl.ds(2 * i, 1), :] = top[2 + i]
-        s_send[pl.ds(2 * i + 1, 1), :] = tot[2 + i]
-    partial = []
-    for n, (src, dst) in enumerate(((s_send, s_recv), (o_send, o_recv))):
-        copy = pltpu.make_async_remote_copy(
-            src, dst, os_send.at[n], os_recv.at[n], device_id=(partner, t), device_id_type=MESH
-        )
-        copy.start()
-        partial.append(copy)
-    for copy in partial:
-        copy.wait_recv()
+        s_send[i, pl.ds(0, 1), :] = top[2 + i]
+        s_send[i, pl.ds(1, 1), :] = tot[2 + i]
+        for n, (src, dst) in enumerate(((s_send, s_recv), (o_send, o_recv))):
+            copy = pltpu.make_async_remote_copy(
+                src.at[i], dst.at[i], os_send.at[i, n], os_recv.at[i, n],
+                device_id=(partner, t), device_id_type=MESH,
+            )
+            copy.start()
+            partial.append(copy)
+    head = y_hi * NX + x
+    rows = att_buf.shape[1]
     for i in range(2):
+        partial[2 * i].wait_recv()
+        partial[2 * i + 1].wait_recv()
         top_one, tot_one = top[i], tot[i]
-        top_two, tot_two = s_recv[pl.ds(2 * i, 1), :], s_recv[pl.ds(2 * i + 1, 1), :]
+        top_two, tot_two = s_recv[i, pl.ds(0, 1), :], s_recv[i, pl.ds(1, 1), :]
         both = jnp.maximum(top_one, top_two)
         one = jnp.exp2((top_one - both) * EXP2_SCALE)
         two = jnp.exp2((top_two - both) * EXP2_SCALE)
         total = tot_one * one + tot_two * two
         merged = (acc[i] * one + o_recv[i].astype(jnp.float32) * two) / total
         att_send[i] = merged.T.astype(jnp.bfloat16)
-
-    head = y_hi * NX + x
-    rows = att_buf.shape[1]
-    for i in range(2):
         for other in range(4):
             src = att_send.at[i, pl.ds(other * rows, rows)]
             mine = (2 * c + i == x) & (t == other)
@@ -259,9 +344,43 @@
             def _():
                 pltpu.make_async_copy(src, att_buf.at[head], d_recv.at[head]).start()
 
-    for h in range(8):
+    for copy in local:
+        copy.wait()
+    wait_bytes(wbuf.at[y_hi * 2 + 1 - c], own_recv)
+    width = 512
+
+    def project(base, columns):
+        total = None
+        for n in range(2):
+            pair = jnp.concatenate([att_buf[base * 4 + 2 * n], att_buf[base * 4 + 2 * n + 1]], axis=1)
+            term = jnp.dot(pair, wbuf[base * 2 + n, :, columns], preferred_element_type=jnp.float32)
+            total = term if total is None else total + term
+        return total
+
+    for n in range(NX):
+        h = y_hi * NX + n
         wait_bytes(att_buf.at[h], d_recv.at[h])
-    att_ref[...] = att_buf[...]
+
+    def first_half(n, carry):
+        columns = pl.ds(pl.multiple_of(n * width, width), width)
+        branch[:, columns] = project(y_hi, columns)
+        return carry
+
+    lax.fori_loop(0, out_ref.shape[1] // width, first_half, 0)
+    for n in range(NX):
+        h = (1 - y_hi) * NX + n
+        wait_bytes(att_buf.at[h], d_recv.at[h])
+    wait_bytes(wbuf.at[(1 - y_hi) * 2 + 1 - c], wsib_recv)
+
+    def second_half(n, carry):
+        columns = pl.ds(pl.multiple_of(n * width, width), width)
+        total = branch[:, columns] + project(1 - y_hi, columns)
+        out_ref[:, columns] = (
+            res[:, columns].astype(jnp.float32) + gate[:, columns] * total
+        ).astype(out_ref.dtype)
+        return carry
+
+    lax.fori_loop(0, out_ref.shape[1] // width, second_half, 0)
 
     for jj in range(2):
         @pl.when(2 * c + jj != x)
@@ -277,6 +396,17 @@
             @pl.when(jnp.logical_not((2 * c + i == x) & (t == other)))
             def _():
                 wait_bytes(att_buf.at[0], d_send.at[i, other])
+    wait_bytes(wbuf.at[0], own_send)
+    wait_bytes(wbuf.at[0], wsib_send)
+    below, above = (x + NX - 1) % NX, (x + 1) % NX
+    for m in range(4):
+        wait_bytes(w_piece(x, m), cross_send.at[m])
+        wait_bytes(w_piece(x, m), x_send.at[0, x * 4 + m])
+        wait_bytes(w_piece(x, m), x_send.at[1, x * 4 + m])
+        if m % 2 == 0:
+            wait_bytes(w_piece(x, m), x_send.at[0, below * 4 + m])
+        else:
+            wait_bytes(w_piece(x, m), x_send.at[1, above * 4 + m])
 
     def drain(h, carry):
         u = h // 2
@@ -305,10 +435,11 @@
     toks = queries.shape[0]
     bf16, f32 = jnp.bfloat16, jnp.float32
     dma = pltpu.SemaphoreType.DMA
-    att = pl.pallas_call(
+    width = residual.shape[1]
+    return pl.pallas_call(
         attention_kernel,
-        out_shape=jax.ShapeDtypeStruct((8, rows, HD), bf16),
-        in_specs=[pl.BlockSpec(memory_space=pl.ANY)] * 4,
+        out_shape=jax.ShapeDtypeStruct((rows, width), bf16),
+        in_specs=[pl.BlockSpec(memory_space=pl.ANY)] * 7,
         out_specs=pl.BlockSpec(memory_space=pltpu.VMEM),
         scratch_shapes=[
             pltpu.SMEM((2, 8, 128), jnp.int32),
@@ -319,23 +450,22 @@
             pltpu.VMEM((4, 1, toks), f32),
             pltpu.VMEM((2, HD, toks), bf16),
             pltpu.VMEM((2, HD, toks), bf16),
-            pltpu.VMEM((8, toks), f32),
-            pltpu.VMEM((8, toks), f32),
+            pltpu.VMEM((2, 8, toks), f32),
+            pltpu.VMEM((2, 8, toks), f32),
             pltpu.VMEM((2, toks, HD), bf16),
             pltpu.VMEM((8, rows, HD), bf16),
+            pltpu.VMEM((4, out_weight.shape[0], width), bf16),
+            pltpu.VMEM((rows, width), bf16),
+            pltpu.VMEM((1, width), f32),
+            pltpu.VMEM((rows, width), f32),
             dma((2,)), dma((2, 3)), dma((2, 3)), dma((2,)), dma((2,)),
             dma((2, HALF)), dma((HALF,)), dma((HALF,)),
-            dma((2,)), dma((2,)), dma((2, 4)), dma((8,)),
+            dma((2, 2)), dma((2, 2)), dma((2, 4)), dma((8,)),
+            dma((3,)), dma((4,)), dma((16,)), dma((2, 16)), dma, dma, dma, dma,
         ],
-        compiler_params=pltpu.CompilerParams(
-            collective_id=0, has_side_effects=True, vmem_limit_bytes=32 * 1024 * 1024
-        ),
+        compiler_params=pltpu.CompilerParams(collective_id=0, has_side_effects=True),
         name="attend",
-    )(queries, keys, values, block_mask)
-    att = jnp.transpose(att, (1, 0, 2)).reshape(rows, 8 * HD)
-    weight = lax.all_gather(out_weight, "tp", axis=0, tiled=True)
-    branch = jnp.dot(att, weight, preferred_element_type=f32)
-    return (residual.astype(f32) + gate[None, :] * branch).astype(bf16)
+    )(queries, keys, values, out_weight, residual, gate.reshape(1, width), block_mask)
 
 
 def solution(mesh):

time: 108 us -> 68.5 us (0.63)
  waiting for transfers between devices: 24.3 us -> 0 us
  between operations: 13.4 us -> 0.01 us
  matrix products: 6.76 us -> 0 us
  Pallas kernels: 63.3 us -> 66.4 us
  local copies, waits for them, and re-layouts: 0.32 us -> 1.97 us
    all_gather x1 -> x0, waiting for transfers between devices: 23.6 us -> none  [shards(): weight = lax.all_gather(out_weight, 'tp', axis=0, tiled=True)]
    dot_general x1 -> x0, matrix products: 6.76 us -> none  [shards(): branch = jnp.dot(att, weight, preferred_element_type=f32)]
    pallas_call x1, Pallas kernels: 63.3 us -> 66.4 us  [shards(): pl.pallas_call(attention_kernel, out_shape=jax.ShapeDtypeStruct((rows, wi...]
    unnamed x12 -> x1, local copies, waits for them, and re-layouts: 0.32 us -> 1.97 us
  transfers between devices with their start and end apart: 1 -> 0, of which waited for: 1 -> 0; matrix products, arithmetic and copies ran while one was open for 0% -> 0% of each run, Pallas kernels for 59% -> 0%
where the time goes in v2:
time: 68.5 us; the launch traced here: 68.3 us
  Pallas kernels  66.4 us (97%)
  local copies, waits for them, and re-layouts  1.97 us (3%)
    pallas_call x1, Pallas kernels, shards(): pl.pallas_call(attention_kernel, out_shape=jax.ShapeDtypeStruct((rows, wi...  66.4 us
    unnamed x1, local copies, waits for them, and re-layouts  1.97 us

profile of v2, /device:TPU:1, one launch (start us, length us, event | category | flops | bytes accessed | tf_op | source)
XLA Modules:
  0.0 68.3 jit_solution(12118487495816427748)
XLA Ops:
  0.0 66.4 %attend.1 = bf16[64,5120]{1,0:T(8,128)(2,1)} custom-call(bf16[256,256]{1,0:T(8,128)(2,1)} %q_ref.1, bf16[256,256]{1,0:T(8,128)(2,1)} %k_ref.1, bf16[256,256]{1,0:T(8,128)(2,1)} %v_ref.1, bf16[256,5120]{1,0:T(8,128)(2,1)} %w_ref.1, bf16[64,5120]{1,0:T(8,128)(2,1)} %res_ref.1, f32[1,5120]{1,0:T(1,128)} %bitcast.1, s32[128,128]{1,0:T(8,128)} %mask_ref.1), custom_call_target="tpu_custom_call" | custom-call | tf_op jit(solution)/shard_map/attend/pallas_call | solution.py:439
  66.4 2.0 %copy.9 = bf16[64,5120]{1,0:T(8,128)(2,1)} copy(bf16[64,5120]{1,0:T(8,128)(2,1)} %attend.1) | data formatting | bytes 1310720

commit v3 on v2

--- a/solution.py
+++ b/solution.py
@@ -20,7 +20,7 @@
 
 
 W_PLAN = (
-    (2, 0, 1), (4, 1, 0), (5, 0, 2), (7, 1, 1), (8, 0, 3), (10, 1, 2), (11, 2, 0), (12, 2, 1), (13, 1, 3),
+    (0, 0, 1), (2, 1, 0), (3, 0, 2), (5, 1, 1), (6, 0, 3), (8, 1, 2), (9, 2, 0), (10, 2, 1), (11, 1, 3),
 )
 
 
@@ -31,7 +31,7 @@
 def attention_kernel(
     q_ref, k_ref, v_ref, w_ref, res_ref, gate_ref, mask_ref, out_ref,
     mask_s, qin, kv, acc, top, tot, o_send, o_recv, s_send, s_recv, att_send, att_buf,
-    wbuf, res, gate, branch,
+    wbuf, res, gate, branch, scores, weights, alphas,
     mask_sem, a_send, a_recv, q_send, q_recv, ring_send, ring_recv, sib_send,
     os_send, os_recv, d_send, d_recv,
     local_sem, cross_send, w_recv, x_send, wsib_send, wsib_recv, own_send, own_recv,
@@ -163,13 +163,18 @@
             device_id=(s, sibling), device_id_type=MESH,
         ).start()
 
-    for e in range(2):
-        idx = z * NX + 2 * c + e
-        for n in range(2):
-            wait_bytes(kv.at[idx, n], a_recv.at[e, n])
-        ring(idx, 0)
-        ring(idx, 1)
-        to_sibling(idx)
+    for n in range(2):
+        for e in range(2):
+            idx = z * NX + 2 * c + e
+            piece = kv.at[idx, n]
+            wait_bytes(piece, a_recv.at[e, n])
+            for goal, sem in (
+                ((z_up, t), ring_send.at[0, idx]), ((z_down, t), ring_send.at[1, idx]),
+                ((s, sibling), sib_send.at[idx]),
+            ):
+                pltpu.make_async_remote_copy(
+                    piece, piece, sem, ring_recv.at[idx], device_id=goal, device_id_type=MESH
+                ).start()
     for i in range(2):
         wait_bytes(qin.at[i], a_recv.at[i, 2])
         pltpu.make_async_remote_copy(
@@ -194,113 +199,111 @@
                     near = near | ((gap <= 2) & (gap >= -2)).astype(jnp.int32)
 
         def one_round(rr, carry):
+            state = []
             for q in range(4):
                 grp, i = q // 2, q % 2
                 row = (2 * c + i) * 2
-                halves_k, halves_v, conds = [], [], []
+                halves_k, uppers, conds = [], [], []
                 for e in range(2):
                     col = 2 * (g0 + e)
                     m00 = mask_s[grp, row, col]
                     m10 = mask_s[grp, row + 1, col]
                     m01 = mask_s[grp, row, col + 1]
                     m11 = mask_s[grp, row + 1, col + 1]
-                    block = (m01 | m11) ^ rr
-                    upper = block != 0
-                    allow0 = jnp.where(upper, m01, m00)
-                    allow1 = jnp.where(upper, m11, m10)
-                    conds.append(jnp.where(lane < BLOCK, allow0, allow1) != 0)
+                    upper = ((m01 | m11) ^ rr) != 0
+                    conds.append((jnp.where(upper, m01, m00), jnp.where(upper, m11, m10)))
+                    uppers.append(upper)
                     halves_k.append(jnp.where(upper, kv[b0 + e, 0, BLOCK:, :], kv[b0 + e, 0, :BLOCK, :]))
-                    halves_v.append(jnp.where(upper, kv[b0 + e, 1, BLOCK:, :], kv[b0 + e, 1, :BLOCK, :]))
-                kk = jnp.concatenate(halves_k, axis=0)
-                vv = jnp.concatenate(halves_v, axis=0)
-                scores = lax.dot_general(
-                    kk, qin[q], (((1,), (1,)), ((), ())), preferred_element_type=jnp.float32
+                scores[q] = lax.dot_general(
+                    jnp.concatenate(halves_k, axis=0), qin[q], (((1,), (1,)), ((), ())),
+                    preferred_element_type=jnp.float32,
                 )
-                parts = (scores[:BLOCK], scores[BLOCK:])
+                state.append((uppers, [jnp.where(lane < BLOCK, *pair) != 0 for pair in conds]))
+            for q in range(4):
+                uppers, conds = state[q]
                 old = top[q]
                 new = old
-                for part, cond in zip(parts, conds):
+                for e, cond in enumerate(conds):
+                    part = scores[q, e * BLOCK:(e + 1) * BLOCK, :]
                     new = jnp.maximum(new, jnp.where(cond, jnp.max(part, axis=0, keepdims=True), LOW))
                 alpha = jnp.exp2((old - new) * EXP2_SCALE)
                 scaled = new * EXP2_SCALE
                 total = tot[q] * alpha
-                weights = []
-                for part, cond in zip(parts, conds):
+                for e, cond in enumerate(conds):
+                    part = scores[q, e * BLOCK:(e + 1) * BLOCK, :]
                     weight = jnp.exp2(part * EXP2_SCALE - jnp.where(cond, scaled, BIG))
                     total = total + jnp.sum(weight, axis=0, keepdims=True)
-                    weights.append(weight.astype(jnp.bfloat16))
+                    weights[q, e * BLOCK:(e + 1) * BLOCK, :] = weight.astype(jnp.bfloat16)
                 top[q] = new
                 tot[q] = total
+                alphas[q] = alpha
+            for q in range(4):
+                uppers, conds = state[q]
+                vv = jnp.concatenate(
+                    [jnp.where(u, kv[b0 + e, 1, BLOCK:, :], kv[b0 + e, 1, :BLOCK, :]) for e, u in enumerate(uppers)],
+                    axis=0,
+                )
                 added = lax.dot_general(
-                    vv, jnp.concatenate(weights, axis=0), (((0,), (0,)), ((), ())),
-                    preferred_element_type=jnp.float32,
+                    vv, weights[q], (((0,), (0,)), ((), ())), preferred_element_type=jnp.float32
                 )
-                acc[q] = acc[q] * alpha + added
+                acc[q] = acc[q] * alphas[q] + added
             return carry
 
         lax.fori_loop(0, 1 + near, one_round, 0)
 
-    def step(h, carry):
-        u = h // 2
-        e = h % 2
-        r = (u + 1) // 2
-        up = (u % 2 == 1).astype(jnp.int32)
+    def arrival(k):
+        r = k // 4 + 1
+        up = (k % 2 == 0).astype(jnp.int32)
+        e = jnp.where(k == 13, 1, (k % 4) // 2)
         zz = (z + NZ + jnp.where(up == 1, -r, r)) % NZ
-        idx = zz * NX + 2 * c + e
-
-        @pl.when(u > 0)
+        return zz * NX + 2 * c + e, (up == 1) & (r < 4 - e), (up == 0) & (r < 3 + e)
+
+    def step(k, carry):
+        @pl.when(k < 14)
         def _():
+            idx, go_up, go_down = arrival(k)
             wait_bytes(kv.at[idx], ring_recv.at[idx])
+            pl.when(go_up)(lambda: ring(idx, 0))
+            pl.when(go_down)(lambda: ring(idx, 1))
             to_sibling(idx)
 
-            @pl.when((up == 1) & (r < 4 - e))
-            def _():
-                ring(idx, 0)
-
-            @pl.when((up == 0) & (r < 3 + e))
-            def _():
-                ring(idx, 1)
-
-        own_rows = pl.ds(pl.multiple_of(h * chunk, 8), chunk)
+        own_rows = pl.ds(pl.multiple_of(k * chunk, 8), chunk)
         pltpu.make_async_remote_copy(
             w_ref.at[own_rows], wbuf.at[t, own_rows], own_send, own_recv,
             device_id=(s, sibling), device_id_type=MESH,
         ).start()
 
         for at, event, m in W_PLAN:
-            @pl.when(h == at)
+            @pl.when(k == at)
             def _():
                 (w_first, w_second, w_third)[event](m)
 
-        @pl.when(h == 1)
+        @pl.when(k == 1)
         def _():
             for i in range(2):
                 wait_bytes(qin.at[2 + i], q_recv.at[i])
 
-        @pl.when(h > 0)
-        def _():
-            pu = jnp.where(e == 0, u - 1, u)
-            pr = (pu + 1) // 2
-            pz = (z + NZ + jnp.where(pu % 2 == 1, -pr, pr)) % NZ
-            pc = jnp.where(e == 0, 1 - c, c)
-
-            @pl.when(e == 0)
+        def pair(p, carry):
+            pr = (p + 2) // 4
+            pz = (z + NZ + jnp.where(p % 2 == 0, -pr, pr)) % NZ
+            other = jnp.where((p < 2) | (p >= 14), p % 2, ((p + 2) // 2) % 2)
+            pc = jnp.where(other == 1, 1 - c, c)
+
+            @pl.when(other == 1)
             def _():
                 for n in range(2):
                     slot = pz * NX + 2 * pc + n
                     wait_bytes(kv.at[slot], ring_recv.at[slot])
 
             compute(pz, pc)
-
+            return carry
+
+        first = jnp.where(k < 4, jnp.maximum(k - 1, 0), k)
+        last = jnp.where(k < 3, k, k + 1)
+        lax.fori_loop(first, last, pair, 0)
         return carry
 
     lax.fori_loop(0, 16, step, 0)
-    last = (z + 4) % NZ
-    for n in range(2):
-        slot = last * NX + 2 * (1 - c) + n
-        wait_bytes(kv.at[slot], ring_recv.at[slot])
-    compute(last, 1 - c)
-
     w_third(2)
     w_third(3)
 
@@ -408,26 +411,19 @@
         else:
             wait_bytes(w_piece(x, m), x_send.at[1, above * 4 + m])
 
-    def drain(h, carry):
-        u = h // 2
-        e = h % 2
-        r = (u + 1) // 2
-        up = (u % 2 == 1).astype(jnp.int32)
-        zz = (z + NZ + jnp.where(up == 1, -r, r)) % NZ
-        idx = zz * NX + 2 * c + e
+    for e in range(2):
+        idx = z * NX + 2 * c + e
+        for sem in (ring_send.at[0, idx], ring_send.at[1, idx], sib_send.at[idx]):
+            wait_bytes(kv.at[idx], sem)
+
+    def drain(k, carry):
+        idx, go_up, go_down = arrival(k)
         wait_bytes(kv.at[idx], sib_send.at[idx])
-
-        @pl.when((u == 0) | ((up == 1) & (r < 4 - e)))
-        def _():
-            wait_bytes(kv.at[idx], ring_send.at[0, idx])
-
-        @pl.when((u == 0) | ((up == 0) & (r < 3 + e)))
-        def _():
-            wait_bytes(kv.at[idx], ring_send.at[1, idx])
-
+        pl.when(go_up)(lambda: wait_bytes(kv.at[idx], ring_send.at[0, idx]))
+        pl.when(go_down)(lambda: wait_bytes(kv.at[idx], ring_send.at[1, idx]))
         return carry
 
-    lax.fori_loop(0, 16, drain, 0)
+    lax.fori_loop(0, 14, drain, 0)
 
 
 def shards(queries, keys, values, out_weight, residual, gate, block_mask):
@@ -458,6 +454,9 @@
             pltpu.VMEM((rows, width), bf16),
             pltpu.VMEM((1, width), f32),
             pltpu.VMEM((rows, width), f32),
+            pltpu.VMEM((4, toks, toks), f32),
+            pltpu.VMEM((4, toks, toks), bf16),
+            pltpu.VMEM((4, 1, toks), f32),
             dma((2,)), dma((2, 3)), dma((2, 3)), dma((2,)), dma((2,)),
             dma((2, HALF)), dma((HALF,)), dma((HALF,)),
             dma((2, 2)), dma((2, 2)), dma((2, 4)), dma((8,)),

time: 68.5 us -> 61.1 us (0.89)
  Pallas kernels: 66.4 us -> 58.9 us
    pallas_call x1, Pallas kernels: 66.4 us -> 58.9 us  [shards(): pl.pallas_call(attention_kernel, out_shape=jax.ShapeDtypeStruct((rows, wi...]
where the time goes in v3:
time: 61.1 us; the launch traced here: 60.9 us
  Pallas kernels  58.9 us (96%)
  local copies, waits for them, and re-layouts  1.97 us (3%)
    pallas_call x1, Pallas kernels, shards(): pl.pallas_call(attention_kernel, out_shape=jax.ShapeDtypeStruct((rows, wi...  58.9 us
    unnamed x1, local copies, waits for them, and re-layouts  1.97 us

profile of v3, /device:TPU:1, one launch (start us, length us, event | category | flops | bytes accessed | tf_op | source)
XLA Modules:
  0.0 60.9 jit_solution(18037236370704918919)
XLA Ops:
  0.0 58.9 %attend.1 = bf16[64,5120]{1,0:T(8,128)(2,1)} custom-call(bf16[256,256]{1,0:T(8,128)(2,1)} %q_ref.1, bf16[256,256]{1,0:T(8,128)(2,1)} %k_ref.1, bf16[256,256]{1,0:T(8,128)(2,1)} %v_ref.1, bf16[256,5120]{1,0:T(8,128)(2,1)} %w_ref.1, bf16[64,5120]{1,0:T(8,128)(2,1)} %res_ref.1, f32[1,5120]{1,0:T(1,128)} %bitcast.1, s32[128,128]{1,0:T(8,128)} %mask_ref.1), custom_call_target="tpu_custom_call" | custom-call | tf_op jit(solution)/shard_map/attend/pallas_call | solution.py:435
  58.9 2.0 %copy.9 = bf16[64,5120]{1,0:T(8,128)(2,1)} copy(bf16[64,5120]{1,0:T(8,128)(2,1)} %attend.1) | data formatting | bytes 1310720

commit v4 on v3

--- a/solution.py
+++ b/solution.py
@@ -20,8 +20,16 @@
 
 
 W_PLAN = (
-    (0, 0, 1), (2, 1, 0), (3, 0, 2), (5, 1, 1), (6, 0, 3), (8, 1, 2), (9, 2, 0), (10, 2, 1), (11, 1, 3),
+    (2, 0, 1), (5, 0, 2), (6, 1, 0), (7, 0, 3), (8, 1, 1), (10, 2, 0), (11, 1, 2), (12, 2, 1), (14, 1, 3),
 )
+
+
+def div(a, b):
+    return lax.div(a, jnp.int32(b))
+
+
+def mod(a, b):
+    return lax.rem(a, jnp.int32(b))
 
 
 def wait_bytes(ref, sem):
@@ -38,17 +46,17 @@
 ):
     s = lax.axis_index("seq")
     t = lax.axis_index("tp")
-    y_lo = s // HALF
-    z = (s // NX) % NZ
-    x = s % NX
-    y_hi = t // 2
-    c = t % 2
+    y_lo = div(s, HALF)
+    z = mod(div(s, NX), NZ)
+    x = mod(s, NX)
+    y_hi = div(t, 2)
+    c = mod(t, 2)
     plane = y_lo * HALF + z * NX
-    z_up = y_lo * HALF + ((z + 1) % NZ) * NX + x
-    z_down = y_lo * HALF + ((z + NZ - 1) % NZ) * NX + x
+    z_up = y_lo * HALF + mod(z + 1, NZ) * NX + x
+    z_down = y_lo * HALF + mod(z + NZ - 1, NZ) * NX + x
     partner = (1 - y_lo) * HALF + z * NX + x
-    x_up = plane + (x + 1) % NX
-    x_down = plane + (x + NX - 1) % NX
+    x_up = plane + mod(x + 1, NX)
+    x_down = plane + mod(x + NX - 1, NX)
     sibling = y_hi * 2 + 1 - c
     facing = (1 - y_hi) * 2 + c
 
@@ -56,9 +64,9 @@
     member = y_hi * 8 + x * 2 + c
 
     def greet(o, carry):
-        m = (member + o) % 16
+        m = mod(member + o, 16)
         pl.semaphore_signal(
-            barrier, inc=1, device_id=(plane + (m // 2) % 4, (m // 8) * 2 + m % 2), device_id_type=MESH
+            barrier, inc=1, device_id=(plane + mod(div(m, 2), 4), div(m, 8) * 2 + mod(m, 2)), device_id_type=MESH
         )
         return carry
 
@@ -84,7 +92,7 @@
     pl.semaphore_wait(barrier, 19)
 
     my_slot = z * NX + x
-    pieces = ((k_ref, kv.at[my_slot, 0]), (v_ref, kv.at[my_slot, 1]), (q_ref, qin.at[x % 2]))
+    pieces = ((k_ref, kv.at[my_slot, 0]), (v_ref, kv.at[my_slot, 1]), (q_ref, qin.at[mod(x, 2)]))
     for jj, n in ((0, 0), (1, 0), (0, 1), (1, 1), (0, 2), (1, 2)):
         j = 2 * c + jj
         src, dst = pieces[n]
@@ -93,13 +101,13 @@
         @pl.when(j != x)
         def _():
             pltpu.make_async_remote_copy(
-                src.at[:, columns], dst, a_send.at[jj, n], a_recv.at[x % 2, n],
-                device_id=(plane + j, y_hi * 2 + x // 2), device_id_type=MESH,
+                src.at[:, columns], dst, a_send.at[jj, n], a_recv.at[mod(x, 2), n],
+                device_id=(plane + j, y_hi * 2 + div(x, 2)), device_id_type=MESH,
             ).start()
 
         @pl.when(j == x)
         def _():
-            pltpu.make_async_copy(src.at[:, columns], dst, a_recv.at[x % 2, n]).start()
+            pltpu.make_async_copy(src.at[:, columns], dst, a_recv.at[mod(x, 2), n]).start()
 
     quarter = w_ref.shape[0] // NX
     chunk = quarter // 4
@@ -136,7 +144,7 @@
         w_sibling(x, m)
 
     def w_second(m):
-        below, above = (x + NX - 1) % NX, (x + 1) % NX
+        below, above = mod(x + NX - 1, NX), mod(x + 1, NX)
         wait_bytes(w_piece(below, m), w_recv.at[below * 4 + m])
         if m % 2 == 0:
             w_to(below, m, 0)
@@ -147,7 +155,7 @@
         w_sibling(above, m)
 
     def w_third(m):
-        far = (x + 2) % NX
+        far = mod(x + 2, NX)
         wait_bytes(w_piece(far, m), w_recv.at[far * 4 + m])
         w_sibling(far, m)
 
@@ -252,10 +260,10 @@
         lax.fori_loop(0, 1 + near, one_round, 0)
 
     def arrival(k):
-        r = k // 4 + 1
-        up = (k % 2 == 0).astype(jnp.int32)
-        e = jnp.where(k == 13, 1, (k % 4) // 2)
-        zz = (z + NZ + jnp.where(up == 1, -r, r)) % NZ
+        r = div(k, 4) + 1
+        up = 1 - mod(k, 2)
+        e = jnp.where(k == 13, 1, div(mod(k, 4), 2))
+        zz = mod(z + NZ + jnp.where(up == 1, -r, r), NZ)
         return zz * NX + 2 * c + e, (up == 1) & (r < 4 - e), (up == 0) & (r < 3 + e)
 
     def step(k, carry):
@@ -284,9 +292,9 @@
                 wait_bytes(qin.at[2 + i], q_recv.at[i])
 
         def pair(p, carry):
-            pr = (p + 2) // 4
-            pz = (z + NZ + jnp.where(p % 2 == 0, -pr, pr)) % NZ
-            other = jnp.where((p < 2) | (p >= 14), p % 2, ((p + 2) // 2) % 2)
+            pr = div(p + 2, 4)
+            pz = mod(z + NZ + jnp.where(mod(p, 2) == 0, -pr, pr), NZ)
+            other = mod(jnp.where((p < 2) | (p >= 14), p, div(p + 2, 2)), 2)
             pc = jnp.where(other == 1, 1 - c, c)
 
             @pl.when(other == 1)
@@ -304,9 +312,6 @@
         return carry
 
     lax.fori_loop(0, 16, step, 0)
-    w_third(2)
-    w_third(3)
-
     partial = []
     for i in range(2):
         o_send[i] = acc[2 + i].astype(jnp.bfloat16)
@@ -319,6 +324,7 @@
             )
             copy.start()
             partial.append(copy)
+    w_third(2)
     head = y_hi * NX + x
     rows = att_buf.shape[1]
     for i in range(2):
@@ -347,44 +353,7 @@
             def _():
                 pltpu.make_async_copy(src, att_buf.at[head], d_recv.at[head]).start()
 
-    for copy in local:
-        copy.wait()
-    wait_bytes(wbuf.at[y_hi * 2 + 1 - c], own_recv)
-    width = 512
-
-    def project(base, columns):
-        total = None
-        for n in range(2):
-            pair = jnp.concatenate([att_buf[base * 4 + 2 * n], att_buf[base * 4 + 2 * n + 1]], axis=1)
-            term = jnp.dot(pair, wbuf[base * 2 + n, :, columns], preferred_element_type=jnp.float32)
-            total = term if total is None else total + term
-        return total
-
-    for n in range(NX):
-        h = y_hi * NX + n
-        wait_bytes(att_buf.at[h], d_recv.at[h])
-
-    def first_half(n, carry):
-        columns = pl.ds(pl.multiple_of(n * width, width), width)
-        branch[:, columns] = project(y_hi, columns)
-        return carry
-
-    lax.fori_loop(0, out_ref.shape[1] // width, first_half, 0)
-    for n in range(NX):
-        h = (1 - y_hi) * NX + n
-        wait_bytes(att_buf.at[h], d_recv.at[h])
-    wait_bytes(wbuf.at[(1 - y_hi) * 2 + 1 - c], wsib_recv)
-
-    def second_half(n, carry):
-        columns = pl.ds(pl.multiple_of(n * width, width), width)
-        total = branch[:, columns] + project(1 - y_hi, columns)
-        out_ref[:, columns] = (
-            res[:, columns].astype(jnp.float32) + gate[:, columns] * total
-        ).astype(out_ref.dtype)
-        return carry
-
-    lax.fori_loop(0, out_ref.shape[1] // width, second_half, 0)
-
+    w_third(3)
     for jj in range(2):
         @pl.when(2 * c + jj != x)
         def _():
@@ -394,14 +363,9 @@
         wait_bytes(qin.at[i], q_send.at[i])
     for copy in partial:
         copy.wait_send()
-    for i in range(2):
-        for other in range(4):
-            @pl.when(jnp.logical_not((2 * c + i == x) & (t == other)))
-            def _():
-                wait_bytes(att_buf.at[0], d_send.at[i, other])
     wait_bytes(wbuf.at[0], own_send)
     wait_bytes(wbuf.at[0], wsib_send)
-    below, above = (x + NX - 1) % NX, (x + 1) % NX
+    below, above = mod(x + NX - 1, NX), mod(x + 1, NX)
     for m in range(4):
         wait_bytes(w_piece(x, m), cross_send.at[m])
         wait_bytes(w_piece(x, m), x_send.at[0, x * 4 + m])
@@ -425,6 +389,50 @@
 
     lax.fori_loop(0, 14, drain, 0)
 
+    for copy in local:
+        copy.wait()
+    wait_bytes(wbuf.at[y_hi * 2 + 1 - c], own_recv)
+    width = 512
+
+    def project(base, columns):
+        total = None
+        for n in range(2):
+            pair = jnp.concatenate([att_buf[base * 4 + 2 * n], att_buf[base * 4 + 2 * n + 1]], axis=1)
+            term = jnp.dot(pair, wbuf[base * 2 + n, :, columns], preferred_element_type=jnp.float32)
+            total = term if total is None else total + term
+        return total
+
+    for n in range(NX):
+        h = y_hi * NX + n
+        wait_bytes(att_buf.at[h], d_recv.at[h])
+
+    def first_half(n, carry):
+        columns = pl.ds(pl.multiple_of(n * width, width), width)
+        branch[:, columns] = project(y_hi, columns)
+        return carry
+
+    lax.fori_loop(0, out_ref.shape[1] // width, first_half, 0)
+    for n in range(NX):
+        h = (1 - y_hi) * NX + n
+        wait_bytes(att_buf.at[h], d_recv.at[h])
+    wait_bytes(wbuf.at[(1 - y_hi) * 2 + 1 - c], wsib_recv)
+
+    def second_half(n, carry):
+        columns = pl.ds(pl.multiple_of(n * width, width), width)
+        total = branch[:, columns] + project(1 - y_hi, columns)
+        out_ref[:, columns] = (
+            res[:, columns].astype(jnp.float32) + gate[:, columns] * total
+        ).astype(out_ref.dtype)
+        return carry
+
+    lax.fori_loop(0, out_ref.shape[1] // width, second_half, 0)
+
+    for i in range(2):
+        for other in range(4):
+            @pl.when(jnp.logical_not((2 * c + i == x) & (t == other)))
+            def _():
+                wait_bytes(att_buf.at[0], d_send.at[i, other])
+
 
 def shards(queries, keys, values, out_weight, residual, gate, block_mask):
     rows = residual.shape[0]
@@ -434,7 +442,7 @@
     width = residual.shape[1]
     return pl.pallas_call(
         attention_kernel,
-        out_shape=jax.ShapeDtypeStruct((rows, width), bf16),
+        out_shape=pltpu.VMEM((rows, width), bf16),
         in_specs=[pl.BlockSpec(memory_space=pl.ANY)] * 7,
         out_specs=pl.BlockSpec(memory_space=pltpu.VMEM),
         scratch_shapes=[

time: 61.1 us -> 58.3 us (0.954)
  Pallas kernels: 58.9 us -> 57.3 us
  local copies, waits for them, and re-layouts: 1.97 us -> 0.84 us
    pallas_call x1, Pallas kernels: 58.9 us -> 57.3 us  [shards(): pl.pallas_call(attention_kernel, out_shape=pltpu.VMEM((rows, width), bf16...]
    unnamed x1, local copies, waits for them, and re-layouts: 1.97 us -> 0.84 us
where the time goes in v4:
time: 58.3 us; the launch traced here: 58.2 us
  Pallas kernels  57.3 us (98%)
  local copies, waits for them, and re-layouts  0.84 us (1%)
    pallas_call x1, Pallas kernels, shards(): pl.pallas_call(attention_kernel, out_shape=pltpu.VMEM((rows, width), bf16...  57.3 us

profile of v4, /device:TPU:1, one launch (start us, length us, event | category | flops | bytes accessed | tf_op | source)
XLA Modules:
  0.0 58.2 jit_solution(607989472673640633)
XLA Ops:
  0.0 57.3 %attend.1 = bf16[64,5120]{1,0:T(8,128)(2,1)S(1)} custom-call(bf16[256,256]{1,0:T(8,128)(2,1)} %q_ref.1, bf16[256,256]{1,0:T(8,128)(2,1)} %k_ref.1, bf16[256,256]{1,0:T(8,128)(2,1)} %v_ref.1, bf16[256,5120]{1,0:T(8,128)(2,1)} %w_ref.1, bf16[64,5120]{1,0:T(8,128)(2,1)} %res_ref.1, f32[1,5120]{1,0:T(1,128)} %bitcast.1, s32[128,128]{1,0:T(8,128)} %mask_ref.1), custom_call_target="tpu_custom_call" | custom-call | tf_op jit(solution)/shard_map/attend/pallas_call | solution.py:443
  57.3 0.8 %copy.9 = bf16[64,5120]{1,0:T(8,128)(2,1)} copy(bf16[64,5120]{1,0:T(8,128)(2,1)S(1)} %attend.1) | data formatting | bytes 1310720

commit v5 on v4

--- a/solution.py
+++ b/solution.py
@@ -20,7 +20,7 @@
 
 
 W_PLAN = (
-    (2, 0, 1), (5, 0, 2), (6, 1, 0), (7, 0, 3), (8, 1, 1), (10, 2, 0), (11, 1, 2), (12, 2, 1), (14, 1, 3),
+    (2, 0, 1), (5, 0, 2), (6, 1, 0), (7, 0, 3), (8, 1, 1), (10, 2, 0), (11, 1, 2), (12, 2, 1),
 )
 
 
@@ -61,16 +61,15 @@
     facing = (1 - y_hi) * 2 + c
 
     barrier = pltpu.get_barrier_semaphore()
-    member = y_hi * 8 + x * 2 + c
-
-    def greet(o, carry):
-        m = mod(member + o, 16)
-        pl.semaphore_signal(
-            barrier, inc=1, device_id=(plane + mod(div(m, 2), 4), div(m, 8) * 2 + mod(m, 2)), device_id_type=MESH
-        )
-        return carry
-
-    lax.fori_loop(1, 16, greet, 0)
+    columns_x = [plane + mod(x + n, NX) for n in range(NX)]
+    chips_t = (y_hi * 2, (1 - y_hi) * 2)
+    for far_hi in (1, 0):
+        for dx in (2, 1, 3, 0):
+            for core in (1 - c, c):
+                if far_hi or dx or core is not c:
+                    pl.semaphore_signal(
+                        barrier, inc=1, device_id=(columns_x[dx], chips_t[far_hi] + core), device_id_type=MESH
+                    )
     for other in (z_up, z_down, partner):
         pl.semaphore_signal(barrier, inc=1, device_id=(other, t), device_id_type=MESH)
     pl.semaphore_signal(barrier, inc=1, device_id=(partner, facing), device_id_type=MESH)
@@ -171,18 +170,25 @@
             device_id=(s, sibling), device_id_type=MESH,
         ).start()
 
-    for n in range(2):
-        for e in range(2):
-            idx = z * NX + 2 * c + e
-            piece = kv.at[idx, n]
-            wait_bytes(piece, a_recv.at[e, n])
-            for goal, sem in (
-                ((z_up, t), ring_send.at[0, idx]), ((z_down, t), ring_send.at[1, idx]),
-                ((s, sibling), sib_send.at[idx]),
-            ):
-                pltpu.make_async_remote_copy(
-                    piece, piece, sem, ring_recv.at[idx], device_id=goal, device_id_type=MESH
-                ).start()
+    def launch(e, n):
+        e = mod(x + e, 2)
+        idx = z * NX + 2 * c + e
+        piece = kv.at[idx, n]
+        wait_bytes(piece, a_recv.at[e, n])
+        for goal, sem in (
+            ((z_up, t), ring_send.at[0, idx]), ((z_down, t), ring_send.at[1, idx]),
+            ((s, sibling), sib_send.at[idx]),
+        ):
+            pltpu.make_async_remote_copy(
+                piece, piece, sem, ring_recv.at[idx], device_id=goal, device_id_type=MESH
+            ).start()
+
+    at_home = div(x, 2) == c
+    launch(0, 0)
+    pl.when(at_home)(lambda: launch(0, 1))
+    launch(1, 0)
+    pl.when(jnp.logical_not(at_home))(lambda: launch(0, 1))
+    launch(1, 1)
     for i in range(2):
         wait_bytes(qin.at[i], a_recv.at[i, 2])
         pltpu.make_async_remote_copy(
@@ -264,7 +270,7 @@
         up = 1 - mod(k, 2)
         e = jnp.where(k == 13, 1, div(mod(k, 4), 2))
         zz = mod(z + NZ + jnp.where(up == 1, -r, r), NZ)
-        return zz * NX + 2 * c + e, (up == 1) & (r < 4 - e), (up == 0) & (r < 3 + e)
+        return zz * NX + 2 * c + mod(x + e, 2), (up == 1) & (r < 4 - e), (up == 0) & (r < 3 + e)
 
     def step(k, carry):
         @pl.when(k < 14)
@@ -306,9 +312,11 @@
             compute(pz, pc)
             return carry
 
-        first = jnp.where(k < 4, jnp.maximum(k - 1, 0), k)
-        last = jnp.where(k < 3, k, k + 1)
-        lax.fori_loop(first, last, pair, 0)
+        def pairs_before(k):
+            ahead = ((k == 12) | (k == 13)).astype(jnp.int32)
+            return jnp.where(k < 4, jnp.maximum(k - 1, 0), k + ahead)
+
+        lax.fori_loop(pairs_before(k), pairs_before(k + 1), pair, 0)
         return carry
 
     lax.fori_loop(0, 16, step, 0)
@@ -324,6 +332,7 @@
             )
             copy.start()
             partial.append(copy)
+    w_second(3)
     w_third(2)
     head = y_hi * NX + x
     rows = att_buf.shape[1]
@@ -335,8 +344,8 @@
         both = jnp.maximum(top_one, top_two)
         one = jnp.exp2((top_one - both) * EXP2_SCALE)
         two = jnp.exp2((top_two - both) * EXP2_SCALE)
-        total = tot_one * one + tot_two * two
-        merged = (acc[i] * one + o_recv[i].astype(jnp.float32) * two) / total
+        share = 1.0 / (tot_one * one + tot_two * two)
+        merged = acc[i] * (one * share) + o_recv[i].astype(jnp.float32) * (two * share)
         att_send[i] = merged.T.astype(jnp.bfloat16)
         for other in range(4):
             src = att_send.at[i, pl.ds(other * rows, rows)]
@@ -392,7 +401,7 @@
     for copy in local:
         copy.wait()
     wait_bytes(wbuf.at[y_hi * 2 + 1 - c], own_recv)
-    width = 512
+    width = 2560
 
     def project(base, columns):
         total = None

time: 58.3 us -> 55.3 us (0.949)
  Pallas kernels: 57.3 us -> 54.3 us
    pallas_call x1, Pallas kernels: 57.3 us -> 54.3 us  [shards(): pl.pallas_call(attention_kernel, out_shape=pltpu.VMEM((rows, width), bf16...]
where the time goes in v5:
time: 55.3 us; the launch traced here: 55.2 us
  Pallas kernels  54.3 us (98%)
  local copies, waits for them, and re-layouts  0.84 us (2%)
    pallas_call x1, Pallas kernels, shards(): pl.pallas_call(attention_kernel, out_shape=pltpu.VMEM((rows, width), bf16...  54.3 us

profile of v5, /device:TPU:1, one launch (start us, length us, event | category | flops | bytes accessed | tf_op | source)
XLA Modules:
  0.0 55.2 jit_solution(2568982507756255223)
XLA Ops:
  0.0 54.3 %attend.1 = bf16[64,5120]{1,0:T(8,128)(2,1)S(1)} custom-call(bf16[256,256]{1,0:T(8,128)(2,1)} %q_ref.1, bf16[256,256]{1,0:T(8,128)(2,1)} %k_ref.1, bf16[256,256]{1,0:T(8,128)(2,1)} %v_ref.1, bf16[256,5120]{1,0:T(8,128)(2,1)} %w_ref.1, bf16[64,5120]{1,0:T(8,128)(2,1)} %res_ref.1, f32[1,5120]{1,0:T(1,128)} %bitcast.1, s32[128,128]{1,0:T(8,128)} %mask_ref.1), custom_call_target="tpu_custom_call" | custom-call | tf_op jit(solution)/shard_map/attend/pallas_call | solution.py:452
  54.3 0.8 %copy.9 = bf16[64,5120]{1,0:T(8,128)(2,1)} copy(bf16[64,5120]{1,0:T(8,128)(2,1)S(1)} %attend.1) | data formatting | bytes 1310720

commit v6 on v5

--- a/solution.py
+++ b/solution.py
@@ -20,7 +20,7 @@
 
 
 W_PLAN = (
-    (2, 0, 1), (5, 0, 2), (6, 1, 0), (7, 0, 3), (8, 1, 1), (10, 2, 0), (11, 1, 2), (12, 2, 1),
+    (1, 0, 1), (3, 0, 2), (5, 1, 0), (6, 0, 3), (7, 1, 1), (9, 2, 0), (9, 1, 2), (11, 2, 1), (12, 1, 3),
 )
 
 
@@ -201,69 +201,67 @@
 
     lane = lax.broadcasted_iota(jnp.int32, (1, 2 * BLOCK), 1)
 
-    def compute(zz, cc):
+    def tiles(zz, cc, rr, queries):
         b0 = zz * NX + 2 * cc
         g0 = y_lo * HALF + b0
-        near = jnp.int32(0)
+        state = {}
+        for q in queries:
+            grp, i = q // 2, q % 2
+            row = (2 * c + i) * 2
+            halves_k, uppers, conds = [], [], []
+            for e in range(2):
+                col = 2 * (g0 + e)
+                m00 = mask_s[grp, row, col]
+                m10 = mask_s[grp, row + 1, col]
+                m01 = mask_s[grp, row, col + 1]
+                m11 = mask_s[grp, row + 1, col + 1]
+                upper = ((m01 | m11) ^ rr) != 0
+                conds.append((jnp.where(upper, m01, m00), jnp.where(upper, m11, m10)))
+                uppers.append(upper)
+                halves_k.append(jnp.where(upper, kv[b0 + e, 0, BLOCK:, :], kv[b0 + e, 0, :BLOCK, :]))
+            scores[q] = lax.dot_general(
+                jnp.concatenate(halves_k, axis=0), qin[q], (((1,), (1,)), ((), ())),
+                preferred_element_type=jnp.float32,
+            )
+            state[q] = (uppers, [jnp.where(lane < BLOCK, *pair) != 0 for pair in conds])
+        for q in queries:
+            uppers, conds = state[q]
+            old = top[q]
+            new = old
+            for e, cond in enumerate(conds):
+                part = scores[q, e * BLOCK:(e + 1) * BLOCK, :]
+                new = jnp.maximum(new, jnp.where(cond, jnp.max(part, axis=0, keepdims=True), LOW))
+            alpha = jnp.exp2((old - new) * EXP2_SCALE)
+            scaled = new * EXP2_SCALE
+            total = tot[q] * alpha
+            for e, cond in enumerate(conds):
+                part = scores[q, e * BLOCK:(e + 1) * BLOCK, :]
+                weight = jnp.exp2(part * EXP2_SCALE - jnp.where(cond, scaled, BIG))
+                total = total + jnp.sum(weight, axis=0, keepdims=True)
+                weights[q, e * BLOCK:(e + 1) * BLOCK, :] = weight.astype(jnp.bfloat16)
+            top[q] = new
+            tot[q] = total
+            alphas[q] = alpha
+        for q in queries:
+            uppers, conds = state[q]
+            vv = jnp.concatenate(
+                [jnp.where(u, kv[b0 + e, 1, BLOCK:, :], kv[b0 + e, 1, :BLOCK, :]) for e, u in enumerate(uppers)],
+                axis=0,
+            )
+            added = lax.dot_general(
+                vv, weights[q], (((0,), (0,)), ((), ())), preferred_element_type=jnp.float32
+            )
+            acc[q] = acc[q] * alphas[q] + added
+
+    def compute(zz, cc):
+        tiles(zz, cc, 0, range(4))
+        g0 = y_lo * HALF + zz * NX + 2 * cc
         for grp, half in enumerate((y_lo, 1 - y_lo)):
-            for i in range(2):
-                a = half * HALF + z * NX + 2 * c + i
-                for e in range(2):
-                    gap = a - (g0 + e)
-                    near = near | ((gap <= 2) & (gap >= -2)).astype(jnp.int32)
-
-        def one_round(rr, carry):
-            state = []
-            for q in range(4):
-                grp, i = q // 2, q % 2
-                row = (2 * c + i) * 2
-                halves_k, uppers, conds = [], [], []
-                for e in range(2):
-                    col = 2 * (g0 + e)
-                    m00 = mask_s[grp, row, col]
-                    m10 = mask_s[grp, row + 1, col]
-                    m01 = mask_s[grp, row, col + 1]
-                    m11 = mask_s[grp, row + 1, col + 1]
-                    upper = ((m01 | m11) ^ rr) != 0
-                    conds.append((jnp.where(upper, m01, m00), jnp.where(upper, m11, m10)))
-                    uppers.append(upper)
-                    halves_k.append(jnp.where(upper, kv[b0 + e, 0, BLOCK:, :], kv[b0 + e, 0, :BLOCK, :]))
-                scores[q] = lax.dot_general(
-                    jnp.concatenate(halves_k, axis=0), qin[q], (((1,), (1,)), ((), ())),
-                    preferred_element_type=jnp.float32,
-                )
-                state.append((uppers, [jnp.where(lane < BLOCK, *pair) != 0 for pair in conds]))
-            for q in range(4):
-                uppers, conds = state[q]
-                old = top[q]
-                new = old
-                for e, cond in enumerate(conds):
-                    part = scores[q, e * BLOCK:(e + 1) * BLOCK, :]
-                    new = jnp.maximum(new, jnp.where(cond, jnp.max(part, axis=0, keepdims=True), LOW))
-                alpha = jnp.exp2((old - new) * EXP2_SCALE)
-                scaled = new * EXP2_SCALE
-                total = tot[q] * alpha
-                for e, cond in enumerate(conds):
-                    part = scores[q, e * BLOCK:(e + 1) * BLOCK, :]
-                    weight = jnp.exp2(part * EXP2_SCALE - jnp.where(cond, scaled, BIG))
-                    total = total + jnp.sum(weight, axis=0, keepdims=True)
-                    weights[q, e * BLOCK:(e + 1) * BLOCK, :] = weight.astype(jnp.bfloat16)
-                top[q] = new
-                tot[q] = total
-                alphas[q] = alpha
-            for q in range(4):
-                uppers, conds = state[q]
-                vv = jnp.concatenate(
-                    [jnp.where(u, kv[b0 + e, 1, BLOCK:, :], kv[b0 + e, 1, :BLOCK, :]) for e, u in enumerate(uppers)],
-                    axis=0,
-                )
-                added = lax.dot_general(
-                    vv, weights[q], (((0,), (0,)), ((), ())), preferred_element_type=jnp.float32
-                )
-                acc[q] = acc[q] * alphas[q] + added
-            return carry
-
-        lax.fori_loop(0, 1 + near, one_round, 0)
+            gap = half * HALF + z * NX + 2 * c - g0
+
+            @pl.when((gap <= 3) & (gap >= -3))
+            def _():
+                tiles(zz, cc, 1, (2 * grp, 2 * grp + 1))
 
     def arrival(k):
         r = div(k, 4) + 1
@@ -319,7 +317,17 @@
         lax.fori_loop(pairs_before(k), pairs_before(k + 1), pair, 0)
         return carry
 
-    lax.fori_loop(0, 16, step, 0)
+    lax.fori_loop(0, 15, step, 0)
+    own_rows = pl.ds(15 * chunk, chunk)
+    pltpu.make_async_remote_copy(
+        w_ref.at[own_rows], wbuf.at[t, own_rows], own_send, own_recv,
+        device_id=(s, sibling), device_id_type=MESH,
+    ).start()
+    last = mod(z + 4, NZ)
+    for n in range(2):
+        slot = last * NX + 2 * (1 - c) + n
+        wait_bytes(kv.at[slot], ring_recv.at[slot])
+    tiles(last, 1 - c, 0, (2, 3))
     partial = []
     for i in range(2):
         o_send[i] = acc[2 + i].astype(jnp.bfloat16)
@@ -332,8 +340,7 @@
             )
             copy.start()
             partial.append(copy)
-    w_second(3)
-    w_third(2)
+    tiles(last, 1 - c, 0, (0, 1))
     head = y_hi * NX + x
     rows = att_buf.shape[1]
     for i in range(2):
@@ -346,7 +353,7 @@
         two = jnp.exp2((top_two - both) * EXP2_SCALE)
         share = 1.0 / (tot_one * one + tot_two * two)
         merged = acc[i] * (one * share) + o_recv[i].astype(jnp.float32) * (two * share)
-        att_send[i] = merged.T.astype(jnp.bfloat16)
+        att_send[i] = merged.astype(jnp.bfloat16).T
         for other in range(4):
             src = att_send.at[i, pl.ds(other * rows, rows)]
             mine = (2 * c + i == x) & (t == other)
@@ -362,6 +369,7 @@
             def _():
                 pltpu.make_async_copy(src, att_buf.at[head], d_recv.at[head]).start()
 
+    w_third(2)
     w_third(3)
     for jj in range(2):
         @pl.when(2 * c + jj != x)

time: 55.3 us -> 54.8 us (level)
  no operation moved by 1% of the time
where the time goes in v6:
time: 54.8 us; the launch traced here: 54.7 us
  Pallas kernels  53.9 us (98%)
  local copies, waits for them, and re-layouts  0.84 us (2%)
    pallas_call x1, Pallas kernels, shards(): pl.pallas_call(attention_kernel, out_shape=pltpu.VMEM((rows, width), bf16...  53.9 us

profile of v6, /device:TPU:1, one launch (start us, length us, event | category | flops | bytes accessed | tf_op | source)
XLA Modules:
  0.0 54.7 jit_solution(14544877672967112697)
XLA Ops:
  0.0 53.9 %attend.1 = bf16[64,5120]{1,0:T(8,128)(2,1)S(1)} custom-call(bf16[256,256]{1,0:T(8,128)(2,1)} %q_ref.1, bf16[256,256]{1,0:T(8,128)(2,1)} %k_ref.1, bf16[256,256]{1,0:T(8,128)(2,1)} %v_ref.1, bf16[256,5120]{1,0:T(8,128)(2,1)} %w_ref.1, bf16[64,5120]{1,0:T(8,128)(2,1)} %res_ref.1, f32[1,5120]{1,0:T(1,128)} %bitcast.1, s32[128,128]{1,0:T(8,128)} %mask_ref.1), custom_call_target="tpu_custom_call" | custom-call | tf_op jit(solution)/shard_map/attend/pallas_call | solution.py:460
  53.9 0.8 %copy.9 = bf16[64,5120]{1,0:T(8,128)(2,1)} copy(bf16[64,5120]{1,0:T(8,128)(2,1)S(1)} %attend.1) | data formatting | bytes 1310720
